TPU v7x, 512 devices: a whole 4x8x8 slice. The times are simulated.
512 devices in a mesh: ep: 64 (over z, x, core), tp: 8 (over y).
Axes of the slice: x: 4, y: 8, z: 8, core: 2. Of those that a mesh axis runs over, the one named last changes fastest.
Arguments:
- attn_out: bfloat16 [8192, 2048], P('ep', 'tp'), may hold values from -6 to 6
- resid: bfloat16 [8192, 2048], P(('ep', 'tp')), may hold values from -6 to 6
- norm_gain: float32 [2048], replicated, may hold values from 0.1 to 1.9
- expert_ids: int32 [8192, 6], P('ep'), may hold values from 0 to 63, all different within a row; in each aligned block of 128 rows (0 to 127, 128 to 255, ...) at most 16 rows name the same one
- gate_vals: float32 [8192, 6], P('ep'), may hold values from 0.1 to 1
- w_gate: bfloat16 [64, 1408, 2048], P('ep', 'tp'), may hold values from -0.125 to 0.125
- w_up: bfloat16 [64, 1408, 2048], P('ep', 'tp'), may hold values from -0.125 to 0.125
- w_down: bfloat16 [64, 1408, 2048], P('ep', 'tp'), may hold values from -0.15625 to 0.15625
Outputs:
- layer_out: bfloat16 [8192, 2048], P(('ep', 'tp'))
Inputs may be any that keep to these rules, and one draw needn't show every extreme that they name: `expert_ids`: among the tokens of one index of ep (aligned blocks of 128 rows), no expert is chosen by more than 16 tokens; some expert reaches 16 in some blocks. The experts of one token differ.
All inputs are finite; a program needn't handle non-finite values.
Results may differ from a plain program's by a relative error of at most 0.0095.
Values may be sent and summed in bfloat16 or wider, within the bound.
A program may use at most 64 MiB of HBM per device.

v0:
```python
import jax
import jax.numpy as jnp
from jax import lax
from jax.sharding import PartitionSpec as P


def by_feature(rows, weight):
    return lax.dot_general(
        rows, weight, (((1,), (1,)), ((), ())), preferred_element_type=jnp.float32
    )


def group_total(partial_rows):
    summed = lax.psum_scatter(
        partial_rows.astype(jnp.float32).astype(jnp.bfloat16), "tp", scatter_dimension=1, tiled=True
    )
    return summed


def all_shares(share_rows):
    return lax.all_gather(share_rows, "tp", axis=1, tiled=True)


def per_device(attn_out, resid, norm_gain, expert_ids, gate_vals, w_gate, w_up, w_down):
    tp_count = lax.axis_size("tp")
    ep_count = lax.axis_size("ep")
    seq_rows = lax.all_to_all(attn_out, "tp", split_axis=0, concat_axis=1, tiled=True)
    hidden_state = (resid.astype(jnp.float32) + seq_rows.astype(jnp.float32)).astype(jnp.bfloat16)
    hidden_f32 = hidden_state.astype(jnp.float32)
    mean_sq = jnp.mean(hidden_f32 * hidden_f32, axis=-1, keepdims=True)
    normed = (hidden_f32 * lax.rsqrt(mean_sq + 1e-05) * norm_gain).astype(jnp.bfloat16)
    normed_all = lax.all_gather(normed, "tp", axis=0, tiled=True)
    tok_block = normed_all.shape[0]
    width = normed_all.shape[1]
    choose_count = expert_ids.shape[1]
    capacity = 4 * tok_block * choose_count // (3 * ep_count)
    flat_ids = expert_ids.reshape(-1)
    onehot = (flat_ids[:, None] == jnp.arange(ep_count, dtype=jnp.int32)[None, :]).astype(jnp.int32)
    rank_in = jnp.sum(onehot * (jnp.cumsum(onehot, axis=0) - onehot), axis=1)
    slot_index = (flat_ids * capacity + rank_in).reshape(tok_block, choose_count)
    slot_range = jnp.arange(ep_count * capacity, dtype=jnp.int32)
    placing = jnp.any(slot_index[None, :, :] == slot_range[:, None, None], axis=-1).astype(
        jnp.bfloat16
    )
    send_rows = jnp.dot(placing, normed_all, preferred_element_type=jnp.float32).astype(
        jnp.bfloat16
    )
    send_rows = send_rows.reshape(ep_count, capacity, width)
    received = lax.all_to_all(send_rows, "ep", split_axis=0, concat_axis=0, tiled=True)
    flat_rows = received.reshape(-1, width)
    gate_pre = by_feature(flat_rows, w_gate[0])
    up_pre = by_feature(flat_rows, w_up[0])
    act = (jax.nn.silu(gate_pre) * up_pre).astype(jnp.bfloat16)
    out_rows = jnp.dot(act, w_down[0], preferred_element_type=jnp.float32).astype(jnp.bfloat16)
    expert_rows = out_rows.reshape(received.shape[0], received.shape[1], width)
    back_rows = lax.all_to_all(expert_rows, "ep", split_axis=0, concat_axis=0, tiled=True)
    slot_rows = all_shares(group_total(back_rows))
    my_rows = tok_block // tp_count
    my_slots = lax.dynamic_slice_in_dim(slot_index, lax.axis_index("tp") * my_rows, my_rows, 0)
    my_gates = lax.dynamic_slice_in_dim(gate_vals, lax.axis_index("tp") * my_rows, my_rows, 0)
    picked = slot_rows.reshape(ep_count * capacity, width)[my_slots]
    moe_rows = jnp.sum(my_gates[:, :, None] * picked.astype(jnp.float32), axis=1)
    return (hidden_f32 + moe_rows).astype(jnp.bfloat16)


def solution(mesh):
    in_specs = (
        P("ep", "tp"),
        P(("ep", "tp"), None),
        P(),
        P("ep", None),
        P("ep", None),
        P("ep", "tp", None),
        P("ep", "tp", None),
        P("ep", "tp", None),
    )
    out_specs = P(("ep", "tp"), None)
    return jax.shard_map(
        per_device, mesh=mesh, in_specs=in_specs, out_specs=out_specs, check_vma=False
    )
```

profile of v0, /device:TPU:1, one launch (start us, length us, event | category | flops | bytes accessed | tf_op | source)
XLA Modules:
  0.0 405.7 jit_solution(2945559172574144904)
XLA Ops:
  6.5 0.0 copy-start
  6.5 7.8 %all-to-all-start = ((bf16[8,16,256]{2,1,0:T(8,128)(2,1)}), bf16[8,16,256]{2,1,0:T(8,128)(2,1)S(1)}, u32[]{:S(2)}, u32[]{:S(2)}) async-start(bf16[8,16,256]{2,1,0:T(8,128)(2,1)} %bitcast.49), calls=%async_computation | async-start | bytes 131072 | tf_op jit(solution)/shard_map/all_to_all | solution.py:27
  14.3 0.0 reduce-scatter.2.cloned.1.call-start
  14.4 0.8 copy.58
  15.1 0.1 eq.42
  15.3 0.1 eq.38
  15.4 1.8 reduce-window.6
  17.2 0.3 slice_reduce_fusion
  17.6 0.1 fusion.15
  17.7 0.1 reduce_sum.30
  17.8 0.1 copy.61
  17.9 0.7 multiply_add_fusion
  18.6 0.5 fusion
  19.1 2.4 all-to-all-done
  21.6 1.0 fusion.17
  22.6 0.8 fusion.19
  23.3 19.3 %all_gather.6 = bf16[128,2048]{1,0:T(8,128)(2,1)S(1)} all-gather(bf16[16,2048]{1,0:T(8,128)(2,1)S(1)} %fusion.19), channel_id=1, replica_groups=mesh['ep'=64,'tp'=8] {'tp'}, dimensions={0}, use_global_device_ids=true | all-gather | bytes 589824 | tf_op jit(solution)/shard_map/all_gather | solution.py:32
  42.6 1.2 convolution_convert_fusion.1
  43.9 0.0 copy-start.3
  43.9 116.2 %all_to_all.23 = bf16[64,16,2048]{2,1,0:T(8,128)(2,1)S(1)} all-to-all(bf16[64,16,2048]{2,1,0:T(8,128)(2,1)S(1)} %bitcast.43), channel_id=1, replica_groups=mesh['ep'=64,'tp'=8] {'ep'}, dimensions={0} | all-to-all | bytes 8388608 | tf_op jit(solution)/shard_map/all_to_all | solution.py:49
  160.1 0.0 copy-start.1
  160.1 0.0 copy-start.4
  160.1 1.9 copy-done.1
  162.0 0.0 copy-done.3
  162.0 2.5 fusion.5
  164.5 0.0 copy-done
  164.5 0.0 copy-done.4
  164.5 7.1 %convolution_convert_fusion = bf16[1024,2048]{1,0:T(8,128)(2,1)} fusion(bf16[1024,2048]{1,0:T(8,128)(2,1)} %bitcast.46, bf16[1,176,2048]{2,1,0:T(8,128)(2,1)S(1)} %copy-done, bf16[1,176,2048]{2,1,0:T(8,128)(2,1)S(1)} %copy-done.4, f32[1024,176]{0,1:T(8,128)} %fusion.5), kind=kOutput, calls=%fused_computation.1 | convolution fusion | flops 1479573504 | bytes 10551296 | tf_op jit(solution)/shard_map/dot_general | solution.py:54
  171.5 101.6 %all_to_all.24 = bf16[64,16,2048]{2,1,0:T(8,128)(2,1)S(1)} all-to-all(bf16[64,16,2048]{2,1,0:T(8,128)(2,1)} %bitcast.47), channel_id=1, replica_groups=mesh['ep'=64,'tp'=8] {'ep'}, dimensions={0} | all-to-all | bytes 8388608 | tf_op jit(solution)/shard_map/all_to_all | solution.py:56
  273.2 4.2 %copy.62 = bf16[64,16,2048]{2,0,1:T(8,128)(2,1)} copy(bf16[64,16,2048]{2,1,0:T(8,128)(2,1)S(1)} %all_to_all.24) | data formatting | bytes 8388608 | tf_op jit(solution)/shard_map/all_to_all | solution.py:56
  277.4 0.0 copy-start.2
  277.4 0.0 reduce-scatter.2.cloned.1.call-update
  277.4 0.2 all-gather.2.cloned.1.call-start
  277.6 51.6 %reduce-scatter.2.cloned.1.call-done = bf16[64,2,2048]{2,0,1:T(8,128)(2,1)} async-done(((bf16[64,16,2048]{2,0,1:T(8,128)(2,1)}), bf16[64,2,2048]{2,0,1:T(8,128)(2,1)}) %reduce-scatter.2.cloned.1.call-update) | async-done | bytes 524304 | tf_op jit(solution)/shard_map/reduce_scatter | solution.py:14
  329.2 0.0 all-gather.2.cloned.1.call-update
  329.2 0.1 compare_select_fusion
  329.3 0.1 copy.64
  329.4 0.1 reshape.61
  329.5 0.0 copy-done.2
  329.5 0.1 constant_dynamic-slice_fusion
  329.6 0.1 copy.57
  329.7 57.7 %all-gather.2.cloned.1.call-done = bf16[64,16,2048]{2,0,1:T(8,128)(2,1)} async-done(((bf16[64,2,2048]{2,0,1:T(8,128)(2,1)}), bf16[64,16,2048]{2,0,1:T(8,128)(2,1)}) %all-gather.2.cloned.1.call-update) | async-done | bytes 4194320 | tf_op jit(solution)/shard_map/all_gather | solution.py:21
  387.3 6.5 %copy.63 = bf16[64,16,2048]{2,1,0:T(8,128)(2,1)} copy(bf16[64,16,2048]{2,0,1:T(8,128)(2,1)} %all-gather.2.cloned.1.call-done) | data formatting | bytes 8388608 | tf_op jit(solution)/shard_map/all_gather | solution.py:21
  393.8 3.9 gather_fusion
  397.7 0.1 reshape.69
  397.8 0.4 multiply_reduce_fusion
  398.2 0.6 fusion.20
  (6 shorter events, 0.1 us)
Async XLA Ops:
  6.5 157.9 %copy-start = (bf16[1,176,2048]{2,1,0:T(8,128)(2,1)S(1)}, bf16[1,176,2048]{2,1,0:T(8,128)(2,1)}, u32[]{:S(2)}) copy-start(bf16[1,176,2048]{2,1,0:T(8,128)(2,1)} %param.15) | copy-start | bytes 2162692
  6.5 15.0 %all-to-all-start = ((bf16[8,16,256]{2,1,0:T(8,128)(2,1)}), bf16[8,16,256]{2,1,0:T(8,128)(2,1)S(1)}, u32[]{:S(2)}, u32[]{:S(2)}) async-start(bf16[8,16,256]{2,1,0:T(8,128)(2,1)} %bitcast.49), calls=%async_computation | async-start | bytes 131072 | tf_op jit(solution)/shard_map/all_to_all | solution.py:27
  14.3 314.9 %reduce-scatter.2.cloned.1.call-start = ((), (), s32[]{:S(2)}) async-start(), calls=%async_computation.4 | async-start | bytes 4718592 | tf_op jit(solution)/shard_map/reduce_scatter | solution.py:14
  43.9 118.1 %copy-start.3 = (bf16[1,176,2048]{2,1,0:T(8,128)(2,1)S(1)}, bf16[1,176,2048]{2,1,0:T(8,128)(2,1)}, u32[]{:S(2)}) copy-start(bf16[1,176,2048]{2,1,0:T(8,128)(2,1)} %param.13) | copy-start | bytes 2162692
  160.1 1.9 copy-start.1
  160.1 4.4 %copy-start.4 = (bf16[1,176,2048]{2,1,0:T(8,128)(2,1)S(1)}, bf16[1,176,2048]{2,1,0:T(8,128)(2,1)}, u32[]{:S(2)}) copy-start(bf16[1,176,2048]{2,1,0:T(8,128)(2,1)} %param.14) | copy-start | bytes 2162692
  277.4 52.1 %copy-start.2 = (f32[128,6]{0,1:T(8,128)S(1)}, f32[128,6]{0,1:T(8,128)}, u32[]{:S(2)}) copy-start(f32[128,6]{0,1:T(8,128)} %param.12) | copy-start | bytes 9220
  277.4 109.9 %all-gather.2.cloned.1.call-start = ((), (), s32[]{:S(2)}) async-start(), calls=%async_computation.5 | async-start | bytes 4718592 | tf_op jit(solution)/shard_map/all_gather | solution.py:21
Sparse Core Ops, SparseCore 0:
  277.5 51.6 reduce-scatter.1
  331.3 56.0 all-gather.1
where the time goes:
time: 406 us
  blocking collectives  237 us (58%)
  waiting for transfers between devices  112 us (28%)
  local copies, waits for them, and re-layouts  18.5 us (5%)
  between operations  13.5 us (3%)
  matrix products  10.8 us (3%)
  starting transfers between devices  8.03 us (2%)
  other arithmetic  6.08 us (1%)
    all_to_all x1, blocking collectives, per_device(): lax.all_to_all(send_rows, 'ep', split_axis=0, concat_axis=0, tiled=True)  116 us
    all_to_all x1, blocking collectives, per_device(): lax.all_to_all(expert_rows, 'ep', split_axis=0, concat_axis=0, tiled=True)  102 us
    all_gather x1, waiting for transfers between devices, all_shares(): return lax.all_gather(share_rows, 'tp', axis=1, tiled=True)  57.7 us
    reduce_scatter x1, waiting for transfers between devices, group_total(): lax.psum_scatter(partial_rows.astype(jnp.float32).astype(jnp.bfloat16), '...  51.6 us
    all_gather x1, blocking collectives, per_device(): normed_all = lax.all_gather(normed, 'tp', axis=0, tiled=True)  19.3 us
  transfers between devices with their start and end apart: 3, of which 3 were waited for; matrix products, arithmetic and copies ran while one was open for 1% of the time, Pallas kernels for 0%

commit v1 on v0

v1 whole, which is shorter than its diff:
```python
import jax
import jax.numpy as jnp
from jax import lax
from jax.sharding import PartitionSpec as P

F32 = jnp.float32
BF16 = jnp.bfloat16


def per_device(attn_out, resid, norm_gain, expert_ids, gate_vals, w_gate, w_up, w_down):
    ep_count = lax.axis_size("ep")
    tok, top = expert_ids.shape
    cap = 4 * tok * top // (3 * ep_count)
    slots = ep_count * cap
    resid_cols = lax.all_to_all(resid, "tp", split_axis=1, concat_axis=0, tiled=True)
    down_cols = lax.all_to_all(w_down[0], "tp", split_axis=1, concat_axis=0, tiled=True)
    h = (resid_cols.astype(F32) + attn_out.astype(F32)).astype(BF16)
    hit = expert_ids[:, :, None] == jnp.arange(ep_count, dtype=jnp.int32)[None, None, :]
    chosen = jnp.any(hit, axis=1).astype(BF16)
    gates = jnp.sum(jnp.where(hit, gate_vals[:, :, None], 0.0), axis=1)
    earlier = jnp.tril(jnp.ones((tok, tok), BF16), -1)
    rank = jnp.dot(earlier, chosen, preferred_element_type=F32).astype(jnp.int32)
    place = (chosen[:, :, None] > 0) & (
        rank[:, :, None] == jnp.arange(cap, dtype=jnp.int32)[None, None, :]
    )
    weights = jnp.where(place, gates[:, :, None], 0.0).reshape(tok, slots)
    place = place.astype(BF16).reshape(tok, slots)
    send = lax.dot_general(place, h, (((0,), (0,)), ((), ())), preferred_element_type=F32).astype(BF16)
    got = lax.all_to_all(send.reshape(ep_count, cap, -1), "ep", split_axis=0, concat_axis=0, tiled=True)
    rows = lax.all_gather(got.reshape(slots, -1), "tp", axis=1, tiled=True)
    rows_f = rows.astype(F32)
    mean_sq = jnp.mean(rows_f * rows_f, axis=-1, keepdims=True)
    normed = (rows_f * lax.rsqrt(mean_sq + 1e-05) * norm_gain).astype(BF16)
    nt = (((1,), (1,)), ((), ()))
    gate_pre = lax.dot_general(w_gate[0], normed, nt, preferred_element_type=F32)
    up_pre = lax.dot_general(w_up[0], normed, nt, preferred_element_type=F32)
    act = (jax.nn.silu(gate_pre) * up_pre).astype(BF16)
    act_all = lax.all_gather(act, "tp", axis=0, tiled=True)
    out = lax.dot_general(
        act_all, down_cols, (((0,), (0,)), ((), ())), preferred_element_type=F32
    ).astype(BF16)
    back = lax.all_to_all(out.reshape(ep_count, cap, -1), "ep", split_axis=0, concat_axis=0, tiled=True)
    moe = jnp.dot(weights, back.reshape(slots, -1).astype(F32), precision=lax.Precision.HIGHEST)
    layer = (h.astype(F32) + moe).astype(BF16)
    return lax.all_to_all(layer, "tp", split_axis=0, concat_axis=1, tiled=True)


def solution(mesh):
    in_specs = (
        P("ep", "tp"),
        P(("ep", "tp"), None),
        P(),
        P("ep", None),
        P("ep", None),
        P("ep", "tp", None),
        P("ep", "tp", None),
        P("ep", "tp", None),
    )
    return jax.shard_map(
        per_device, mesh=mesh, in_specs=in_specs, out_specs=P(("ep", "tp"), None), check_vma=False
    )
```

time: 406 us -> 220 us (0.54)
  blocking collectives: 237 us -> 63.2 us
  local copies, waits for them, and re-layouts: 18.5 us -> 2.79 us
  starting transfers between devices: 8.03 us -> 18.4 us
    all_to_all x2 -> x3, blocking collectives: 218 us -> 63.2 us  [the longest x1 33 us: per_device(): lax.all_to_all(send.reshape(ep_count, cap, -1), 'ep', split_axis=0, conca...]
    reduce_scatter x1 -> x0, waiting for transfers between devices: 51.6 us -> none  [group_total(): lax.psum_scatter(partial_rows.astype(jnp.float32).astype(jnp.bfloat16), '...]
    all_gather x1 -> x2, waiting for transfers between devices: 57.7 us -> 84 us  [the longest x1 52.2 us: per_device(): rows = lax.all_gather(got.reshape(slots, -1), 'tp', axis=1, tiled=True)]
    all_to_all x1 -> x2, waiting for transfers between devices: 2.42 us -> 23.6 us  [the longest x1 17.6 us: per_device(): lax.all_to_all(out.reshape(ep_count, cap, -1), 'ep', split_axis=0, concat...]
    all_gather x1 -> x0, blocking collectives: 19.3 us -> none  [per_device(): normed_all = lax.all_gather(normed, 'tp', axis=0, tiled=True)]
    all_to_all x1 -> x2, starting transfers between devices: 7.77 us -> 18.3 us  [the longest x1 10.7 us: per_device(): lax.all_to_all(out.reshape(ep_count, cap, -1), 'ep', split_axis=0, concat...]
    all_gather x1 -> x0, local copies, waits for them, and re-layouts: 6.45 us -> none  [all_shares(): return lax.all_gather(share_rows, 'tp', axis=1, tiled=True)]
    dot_general x3 -> x6, matrix products: 10.8 us -> 9 us  [the longest x1 3.65 us: per_device(): lax.dot_general(act_all, down_cols, (((0,), (0,)), ((), ())), preferred_e...]
  transfers between devices with their start and end apart: 3 -> 4, of which waited for: 3 -> 4; matrix products, arithmetic and copies ran while one was open for 1% -> 1% of each run, Pallas kernels for 0% -> 0%
where the time goes in v1:
time: 220 us
  waiting for transfers between devices  108 us (49%)
  blocking collectives  63.2 us (29%)
  starting transfers between devices  18.4 us (8%)
  between operations  13.6 us (6%)
  matrix products  9 us (4%)
  other arithmetic  5.07 us (2%)
  local copies, waits for them, and re-layouts  2.79 us (1%)
    all_gather x1, waiting for transfers between devices, per_device(): rows = lax.all_gather(got.reshape(slots, -1), 'tp', axis=1, tiled=True)  52.2 us
    all_to_all x1, blocking collectives, per_device(): lax.all_to_all(send.reshape(ep_count, cap, -1), 'ep', split_axis=0, conca...  33 us
    all_gather x1, waiting for transfers between devices, per_device(): act_all = lax.all_gather(act, 'tp', axis=0, tiled=True)  31.8 us
    all_to_all x1, blocking collectives, per_device(): lax.all_to_all(w_down[0], 'tp', split_axis=1, concat_axis=0, tiled=True)  19.1 us
    all_to_all x1, waiting for transfers between devices, per_device(): lax.all_to_all(out.reshape(ep_count, cap, -1), 'ep', split_axis=0, concat...  17.6 us
    all_to_all x1, blocking collectives, per_device(): return lax.all_to_all(layer, 'tp', split_axis=0, concat_axis=1, tiled=True)  11.1 us
    all_to_all x1, starting transfers between devices, per_device(): lax.all_to_all(out.reshape(ep_count, cap, -1), 'ep', split_axis=0, concat...  10.7 us
    all_to_all x1, starting transfers between devices, per_device(): lax.all_to_all(resid, 'tp', split_axis=1, concat_axis=0, tiled=True)  7.64 us
  transfers between devices with their start and end apart: 4, of which 4 were waited for; matrix products, arithmetic and copies ran while one was open for 1% of the time, Pallas kernels for 0%

profile of v1, /device:TPU:1, one launch (start us, length us, event | category | flops | bytes accessed | tf_op | source)
XLA Modules:
  0.0 219.6 jit_solution(954548781873976257)
XLA Ops:
  6.5 0.0 copy-start
  6.5 0.0 copy-start.6
  6.5 1.5 copy.37
  8.1 7.6 %all-to-all-start = ((bf16[16,8,256]{2,0,1:T(8,128)(2,1)}), bf16[16,8,256]{2,0,1:T(8,128)(2,1)S(1)}, u32[]{:S(2)}, u32[]{:S(2)}) async-start(bf16[16,8,256]{2,0,1:T(8,128)(2,1)} %bitcast.54), calls=%async_computation | async-start | bytes 131072 | tf_op jit(solution)/shard_map/all_to_all | solution.py:15
  15.7 0.0 all-gather.3.cloned.1.call-start
  15.8 0.7 fusion.19
  16.5 0.1 eq.45
  16.6 0.2 convolution_convert_fusion.2
  16.8 0.2 fusion.14
  17.0 5.9 %all-to-all-done = bf16[16,8,256]{2,0,1:T(8,128)(2,1)S(1)} async-done(((bf16[16,8,256]{2,0,1:T(8,128)(2,1)}), bf16[16,8,256]{2,0,1:T(8,128)(2,1)S(1)}, u32[]{:S(2)}, u32[]{:S(2)}) %all-to-all-start) | async-done | bytes 65568 | tf_op jit(solution)/shard_map/all_to_all | solution.py:15
  22.9 0.9 fusion.20
  23.8 0.3 convolution_convert_fusion.1
  24.1 33.0 %all_to_all.61 = bf16[64,16,256]{2,1,0:T(8,128)(2,1)} all-to-all(bf16[64,16,256]{2,1,0:T(8,128)(2,1)S(1)} %bitcast.57), channel_id=1, replica_groups=mesh['ep'=64,'tp'=8] {'ep'}, dimensions={0} | all-to-all | bytes 1048576 | tf_op jit(solution)/shard_map/all_to_all | solution.py:29
  57.1 0.0 all-gather.3.cloned.1.call-update
  57.2 0.0 all-gather.5.cloned.1.call-start
  57.2 52.2 %all-gather.3.cloned.1.call-done = bf16[1024,2048]{1,0:T(8,128)(2,1)} async-done(((bf16[1024,256]{1,0:T(8,128)(2,1)}), bf16[1024,2048]{1,0:T(8,128)(2,1)}) %all-gather.3.cloned.1.call-update) | async-done | bytes 4194320 | tf_op jit(solution)/shard_map/all_gather | solution.py:30
  109.4 0.0 copy-start.1
  109.4 3.2 %fusion = f32[1024]{0:T(1024)S(1)} fusion(bf16[1024,2048]{1,0:T(8,128)(2,1)} %all-gather.3.cloned.1.call-done), kind=kLoop, calls=%fused_computation.2 | loop fusion | flops 6290432 | bytes 4198400 | tf_op jit(solution)/shard_map/reduce_sum | solution.py:32
  112.7 0.0 copy-done
  112.7 0.0 copy-done.6
  112.7 0.2 copy-done.1
  112.9 0.0 copy-start.5
  112.9 1.7 convolution_bitcast_fusion.1
  114.5 0.0 copy-done.5
  114.6 0.0 copy-start.2
  114.6 2.6 %fusion.4 = bf16[176,1024]{1,0:T(8,128)(2,1)} fusion(bf16[1024,2048]{1,0:T(8,128)(2,1)S(1)} %copy-done.1, f32[2048]{0:T(1024)S(1)} %copy-done.6, f32[1024]{0:T(1024)S(1)} %add_rsqrt_fusion, bf16[1,176,2048]{2,1,0:T(8,128)(2,1)S(1)} %copy-done.5, f32[176,1024]{1,0:T(8,128)S(1)} %convolution_bitcast_fusion.1), kind=kOutput, calls=%fused_computation.10 | convolution fusion | flops 747667456 | bytes 6008832 | tf_op jit(solution)/shard_map/dot_general | solution.py:36
  117.1 0.0 all-gather.5.cloned.1.call-update
  117.2 0.0 copy-done.2
  117.2 0.2 copy.35
  117.4 0.1 copy.31
  117.5 0.0 copy-start.3
  117.5 0.0 copy-start.4
  117.5 19.1 %all_to_all.62 = bf16[176,8,256]{2,0,1:T(8,128)(2,1)S(1)} all-to-all(bf16[176,8,256]{2,0,1:T(8,128)(2,1)S(1)} %copy.31), channel_id=1, replica_groups=mesh['ep'=64,'tp'=8] {'tp'}, dimensions={1} | all-to-all | bytes 1441792 | tf_op jit(solution)/shard_map/all_to_all | solution.py:16
  136.6 31.8 %all-gather.5.cloned.1.call-done = bf16[1408,1024]{1,0:T(8,128)(2,1)} async-done(((bf16[176,1024]{1,0:T(8,128)(2,1)}), bf16[1408,1024]{1,0:T(8,128)(2,1)}) %all-gather.5.cloned.1.call-update) | async-done | bytes 2883600 | tf_op jit(solution)/shard_map/all_gather | solution.py:38
  168.4 3.6 %convolution_convert_fusion = bf16[1024,256]{1,0:T(8,128)(2,1)} fusion(bf16[1408,1024]{1,0:T(8,128)(2,1)} %all-gather.5.cloned.1.call-done, bf16[1408,256]{1,0:T(8,128)(2,1)S(1)} %bitcast.59), kind=kOutput, calls=%fused_computation.5 | convolution fusion | flops 738459648 | bytes 4128768 | tf_op jit(solution)/shard_map/dot_general | solution.py:39
  172.1 10.7 %all-to-all-start.3 = ((bf16[64,16,256]{2,1,0:T(8,128)(2,1)}), bf16[64,16,256]{2,1,0:T(8,128)(2,1)S(1)}, u32[]{:S(2)}, u32[]{:S(2)}) async-start(bf16[64,16,256]{2,1,0:T(8,128)(2,1)} %bitcast.12), calls=%async_computation.3 | async-start | bytes 1048576 | tf_op jit(solution)/shard_map/all_to_all | solution.py:42
  182.8 0.0 copy-done.3
  182.8 0.0 copy-done.4
  182.8 17.6 %all-to-all-done.3 = bf16[64,16,256]{2,1,0:T(8,128)(2,1)S(1)} async-done(((bf16[64,16,256]{2,1,0:T(8,128)(2,1)}), bf16[64,16,256]{2,1,0:T(8,128)(2,1)S(1)}, u32[]{:S(2)}, u32[]{:S(2)}) %all-to-all-start.3) | async-done | bytes 524320 | tf_op jit(solution)/shard_map/all_to_all | solution.py:42
  200.5 0.6 fusion.8
  201.1 11.1 %all_to_all.63 = bf16[8,16,256]{2,1,0:T(8,128)(2,1)S(1)} all-to-all(bf16[8,16,256]{2,1,0:T(8,128)(2,1)S(1)} %bitcast.62), channel_id=1, replica_groups=mesh['ep'=64,'tp'=8] {'tp'}, dimensions={0} | all-to-all | bytes 131072 | tf_op jit(solution)/shard_map/all_to_all | solution.py:45
  212.2 0.6 copy.34
  (5 shorter events, 0.1 us)
Async XLA Ops:
  6.5 106.1 %copy-start = (bf16[1,176,2048]{2,1,0:T(8,128)(2,1)S(1)}, bf16[1,176,2048]{2,1,0:T(8,128)(2,1)}, u32[]{:S(2)}) copy-start(bf16[1,176,2048]{2,1,0:T(8,128)(2,1)} %param.13) | copy-start | bytes 2162692
  6.5 106.1 %copy-start.6 = (f32[2048]{0:T(1024)S(1)}, f32[2048]{0:T(1024)}, u32[]{:S(2)}) copy-start(f32[2048]{0:T(1024)} %param.10) | copy-start | bytes 24580
  8.1 14.9 %all-to-all-start = ((bf16[16,8,256]{2,0,1:T(8,128)(2,1)}), bf16[16,8,256]{2,0,1:T(8,128)(2,1)S(1)}, u32[]{:S(2)}, u32[]{:S(2)}) async-start(bf16[16,8,256]{2,0,1:T(8,128)(2,1)} %bitcast.54), calls=%async_computation | async-start | bytes 131072 | tf_op jit(solution)/shard_map/all_to_all | solution.py:15
  15.7 93.7 %all-gather.3.cloned.1.call-start = ((), (), s32[]{:S(2)}) async-start(), calls=%async_computation.5 | async-start | bytes 4718592 | tf_op jit(solution)/shard_map/all_gather | solution.py:30
  57.2 111.3 %all-gather.5.cloned.1.call-start = ((), (), s32[]{:S(2)}) async-start(), calls=%async_computation.6 | async-start | bytes 3244032 | tf_op jit(solution)/shard_map/all_gather | solution.py:38
  109.4 3.4 %copy-start.1 = (bf16[1024,2048]{1,0:T(8,128)(2,1)S(1)}, bf16[1024,2048]{1,0:T(8,128)(2,1)}, u32[]{:S(2)}) copy-start(bf16[1024,2048]{1,0:T(8,128)(2,1)} %all-gather.3.cloned.1.call-done) | copy-start | bytes 12582916
  112.9 1.7 copy-start.5
  114.6 2.6 %copy-start.2 = (bf16[1,176,2048]{2,1,0:T(8,128)(2,1)S(1)}, bf16[1,176,2048]{2,1,0:T(8,128)(2,1)}, u32[]{:S(2)}) copy-start(bf16[1,176,2048]{2,1,0:T(8,128)(2,1)} %param.15) | copy-start | bytes 2162692
  117.5 65.3 %copy-start.3 = (s32[128,6]{0,1:T(8,128)S(1)}, s32[128,6]{0,1:T(8,128)}, u32[]{:S(2)}) copy-start(s32[128,6]{0,1:T(8,128)} %param.11) | copy-start | bytes 9220
  117.5 65.3 %copy-start.4 = (f32[128,6]{0,1:T(8,128)S(1)}, f32[128,6]{0,1:T(8,128)}, u32[]{:S(2)}) copy-start(f32[128,6]{0,1:T(8,128)} %param.12) | copy-start | bytes 9220
  172.1 28.4 %all-to-all-start.3 = ((bf16[64,16,256]{2,1,0:T(8,128)(2,1)}), bf16[64,16,256]{2,1,0:T(8,128)(2,1)S(1)}, u32[]{:S(2)}, u32[]{:S(2)}) async-start(bf16[64,16,256]{2,1,0:T(8,128)(2,1)} %bitcast.12), calls=%async_computation.3 | async-start | bytes 1048576 | tf_op jit(solution)/shard_map/all_to_all | solution.py:42
Sparse Core Ops, SparseCore 0:
  57.3 52.0 all-gather.2
  117.3 51.0 all-gather.4

commit v2 on v1

--- a/solution.py
+++ b/solution.py
@@ -1,14 +1,133 @@
+import functools
+
 import jax
 import jax.numpy as jnp
 from jax import lax
+from jax.experimental import pallas as pl
+from jax.experimental.pallas import tpu as pltpu
 from jax.sharding import PartitionSpec as P
 
 F32 = jnp.float32
 BF16 = jnp.bfloat16
+MESH = pl.DeviceIdType.MESH
+NT = (((1,), (1,)), ((), ()))
+TN = (((0,), (0,)), ((), ()))
+
+
+def ring_kernel(n, got, w_gate, w_up, w_down, gain, out, rows, acts, own_act, gate_acc, up_acc, sq_acc, out_acc,
+                row_send, row_recv, act_send, act_recv):
+    me = lax.axis_index("tp")
+    after, before = lax.rem(me + 1, n), lax.rem(me + n - 1, n)
+    half = n // 2
+    width = got.shape[2]
+
+    barrier = pltpu.get_barrier_semaphore()
+    for neighbour in (before, after):
+        pl.semaphore_signal(barrier, inc=1, device_id={"tp": neighbour}, device_id_type=MESH)
+    pl.semaphore_wait(barrier, 2)
+
+    def origin(way, hop):
+        return lax.rem(me + n - hop, n) if way == 0 else lax.rem(me + hop, n)
+
+    def copy(first, buf, send_sem, recv_sem, way, hop, chunk):
+        src = first.at[chunk] if hop == 0 else buf.at[way, hop - 1, chunk]
+        return pltpu.make_async_remote_copy(
+            src_ref=src,
+            dst_ref=buf.at[way, hop, chunk],
+            send_sem=send_sem.at[way, hop, chunk],
+            recv_sem=recv_sem.at[way, hop, chunk],
+            device_id={"tp": after if way == 0 else before},
+            device_id_type=MESH,
+        )
+
+    def travels(way, hop, chunk):
+        return hop < half - 1 or (hop == half - 1 and chunk == way)
+
+    def gather(first, buf, send_sem, recv_sem, use):
+        make = functools.partial(copy, first, buf, send_sem, recv_sem)
+        steps = [(way, chunk) for turn in range(2) for way, chunk in ((0, turn), (1, 1 - turn))]
+        for way, chunk in steps:
+            make(way, 0, chunk).start()
+        use(first, me, (0, 1))
+        for hop in range(1, half + 1):
+            for pair in (steps[:2], steps[2:]):
+                landed = [(way, chunk) for way, chunk in pair if travels(way, hop - 1, chunk)]
+                for way, chunk in landed:
+                    make(way, hop - 1, chunk).wait_recv()
+                    if travels(way, hop, chunk):
+                        make(way, hop, chunk).start()
+                for way, chunk in landed:
+                    use(buf.at[way, hop - 1], origin(way, hop), (chunk,))
+        for hop in range(half):
+            for way, chunk in steps:
+                if travels(way, hop, chunk):
+                    make(way, hop, chunk).wait_send()
+
+    gate_acc[...] = jnp.zeros_like(gate_acc)
+    up_acc[...] = jnp.zeros_like(up_acc)
+    sq_acc[...] = jnp.zeros_like(sq_acc)
+    ones = jnp.ones((8, width), BF16)
+
+    def project(block, src, chunks):
+        columns = pl.ds(pl.multiple_of(src * width, width), width)
+        scale = gain[:, columns]
+        gate_w = (w_gate[:, columns].astype(F32) * scale).astype(BF16)
+        up_w = (w_up[:, columns].astype(F32) * scale).astype(BF16)
+        for c in chunks:
+            x = block[c]
+            gate_acc[c] += lax.dot_general(gate_w, x, NT, preferred_element_type=F32)
+            up_acc[c] += lax.dot_general(up_w, x, NT, preferred_element_type=F32)
+            sq = x.astype(F32) * x.astype(F32)
+            top = sq.astype(BF16)
+            rest = (sq - top.astype(F32)).astype(BF16)
+            sq_acc[c] += lax.dot_general(ones, top, NT, preferred_element_type=F32) + lax.dot_general(
+                ones, rest, NT, preferred_element_type=F32)
+
+    gather(got, rows, row_send, row_recv, project)
+
+    for c in range(2):
+        r = lax.rsqrt(sq_acc[c][:1] / (n * width) + 1e-05)
+        g = gate_acc[c] * r
+        own_act[c] = (g / (1.0 + jnp.exp(-g)) * (up_acc[c] * r)).astype(BF16)
+    out_acc[...] = jnp.zeros_like(out_acc)
+
+    def reduce(block, src, chunks):
+        w = w_down[src]
+        for c in chunks:
+            out_acc[c] += lax.dot_general(block[c], w, TN, preferred_element_type=F32)
+
+    gather(own_act, acts, act_send, act_recv, reduce)
+    out[...] = out_acc[...].astype(BF16)
+
+
+def experts(n, got, w_gate, w_up, w_down, gain):
+    _, part, width = got.shape
+    hidden = w_gate.shape[0]
+    half = n // 2
+    vmem = pl.BlockSpec(memory_space=pltpu.VMEM)
+    sems = pltpu.SemaphoreType.DMA((2, half, 2))
+    return pl.pallas_call(
+        functools.partial(ring_kernel, n),
+        out_shape=jax.ShapeDtypeStruct(got.shape, BF16),
+        in_specs=[vmem] * 5,
+        out_specs=vmem,
+        scratch_shapes=[
+            pltpu.VMEM((2, half, 2, part, width), BF16),
+            pltpu.VMEM((2, half, 2, hidden, part), BF16),
+            pltpu.VMEM((2, hidden, part), BF16),
+            pltpu.VMEM((2, hidden, part), F32),
+            pltpu.VMEM((2, hidden, part), F32),
+            pltpu.VMEM((2, 8, part), F32),
+            pltpu.VMEM((2, part, width), F32),
+            sems, sems, sems, sems,
+        ],
+        compiler_params=pltpu.CompilerParams(collective_id=0, has_side_effects=True, vmem_limit_bytes=40 * 2**20),
+    )(got, w_gate, w_up, w_down, gain)
 
 
 def per_device(attn_out, resid, norm_gain, expert_ids, gate_vals, w_gate, w_up, w_down):
     ep_count = lax.axis_size("ep")
+    tp_count = lax.axis_size("tp")
     tok, top = expert_ids.shape
     cap = 4 * tok * top // (3 * ep_count)
     slots = ep_count * cap
@@ -27,18 +146,14 @@
     place = place.astype(BF16).reshape(tok, slots)
     send = lax.dot_general(place, h, (((0,), (0,)), ((), ())), preferred_element_type=F32).astype(BF16)
     got = lax.all_to_all(send.reshape(ep_count, cap, -1), "ep", split_axis=0, concat_axis=0, tiled=True)
-    rows = lax.all_gather(got.reshape(slots, -1), "tp", axis=1, tiled=True)
-    rows_f = rows.astype(F32)
-    mean_sq = jnp.mean(rows_f * rows_f, axis=-1, keepdims=True)
-    normed = (rows_f * lax.rsqrt(mean_sq + 1e-05) * norm_gain).astype(BF16)
-    nt = (((1,), (1,)), ((), ()))
-    gate_pre = lax.dot_general(w_gate[0], normed, nt, preferred_element_type=F32)
-    up_pre = lax.dot_general(w_up[0], normed, nt, preferred_element_type=F32)
-    act = (jax.nn.silu(gate_pre) * up_pre).astype(BF16)
-    act_all = lax.all_gather(act, "tp", axis=0, tiled=True)
-    out = lax.dot_general(
-        act_all, down_cols, (((0,), (0,)), ((), ())), preferred_element_type=F32
-    ).astype(BF16)
+    out = experts(
+        tp_count,
+        got.reshape(2, slots // 2, -1),
+        w_gate[0],
+        w_up[0],
+        down_cols.reshape(tp_count, w_down.shape[1], -1),
+        norm_gain[None, :],
+    )
     back = lax.all_to_all(out.reshape(ep_count, cap, -1), "ep", split_axis=0, concat_axis=0, tiled=True)
     moe = jnp.dot(weights, back.reshape(slots, -1).astype(F32), precision=lax.Precision.HIGHEST)
     layer = (h.astype(F32) + moe).astype(BF16)

time: 220 us -> 186 us (0.85)
  Pallas kernels: 0 us -> 72 us
  waiting for transfers between devices: 108 us -> 41.6 us
  blocking collectives: 63.2 us -> 35.8 us
  between operations: 13.6 us -> 0.16 us
  starting transfers between devices: 18.4 us -> 30.5 us
  matrix products: 9 us -> 1.9 us
  other arithmetic: 5.07 us -> 0.31 us
    all_gather x2 -> x0, waiting for transfers between devices: 84 us -> none  [the longest x1 52.2 us: per_device(): rows = lax.all_gather(got.reshape(slots, -1), 'tp', axis=1, tiled=True)]
    pallas_call x0 -> x1, Pallas kernels: none -> 72 us  [experts(): pl.pallas_call(functools.partial(ring_kernel, n), out_shape=jax.ShapeDtyp...]
    all_to_all x1 -> x0, blocking collectives: 33 us -> none  [per_device(): lax.all_to_all(send.reshape(ep_count, cap, -1), 'ep', split_axis=0, conca...]
    all_to_all x0 -> x1, waiting for transfers between devices: none -> 17.3 us  [per_device(): lax.all_to_all(send.reshape(ep_count, cap, -1), 'ep', split_axis=0, conca...]
    all_to_all x0 -> x1, starting transfers between devices: none -> 15.4 us  [per_device(): lax.all_to_all(send.reshape(ep_count, cap, -1), 'ep', split_axis=0, conca...]
    dot_general x3 -> x0, matrix products: 7.89 us -> none  [the longest x1 3.65 us: per_device(): lax.dot_general(act_all, down_cols, (((0,), (0,)), ((), ())), preferred_e...]
    all_to_all x1, blocking collectives: 19.1 us -> 24.5 us  [per_device(): lax.all_to_all(w_down[0], 'tp', split_axis=1, concat_axis=0, tiled=True)]
    all_to_all x1, starting transfers between devices: 10.7 us -> 7.29 us  [per_device(): lax.all_to_all(out.reshape(ep_count, cap, -1), 'ep', split_axis=0, concat...]
  transfers between devices with their start and end apart: 4 -> 3, of which waited for: 4 -> 3; matrix products, arithmetic and copies ran while one was open for 1% -> 0% of each run, Pallas kernels for 0% -> 0%
where the time goes in v2:
time: 186 us; the launch traced here: 185 us
  Pallas kernels  72 us (39%)
  waiting for transfers between devices  41.6 us (22%)
  blocking collectives  35.8 us (19%)
  starting transfers between devices  30.5 us (16%)
  local copies, waits for them, and re-layouts  3.23 us (2%)
  matrix products  1.9 us (1%)
    pallas_call x1, Pallas kernels, experts(): pl.pallas_call(functools.partial(ring_kernel, n), out_shape=jax.ShapeDtyp...  72 us
    all_to_all x1, blocking collectives, per_device(): lax.all_to_all(w_down[0], 'tp', split_axis=1, concat_axis=0, tiled=True)  24.5 us
    all_to_all x1, waiting for transfers between devices, per_device(): lax.all_to_all(out.reshape(ep_count, cap, -1), 'ep', split_axis=0, concat...  17.6 us
    all_to_all x1, waiting for transfers between devices, per_device(): lax.all_to_all(send.reshape(ep_count, cap, -1), 'ep', split_axis=0, conca...  17.3 us
    all_to_all x1, starting transfers between devices, per_device(): lax.all_to_all(send.reshape(ep_count, cap, -1), 'ep', split_axis=0, conca...  15.4 us
    all_to_all x1, blocking collectives, per_device(): return lax.all_to_all(layer, 'tp', split_axis=0, concat_axis=1, tiled=True)  11.2 us
    all_to_all x1, starting transfers between devices, per_device(): lax.all_to_all(resid, 'tp', split_axis=1, concat_axis=0, tiled=True)  7.77 us
    all_to_all x1, starting transfers between devices, per_device(): lax.all_to_all(out.reshape(ep_count, cap, -1), 'ep', split_axis=0, concat...  7.29 us
  transfers between devices with their start and end apart: 3, of which 3 were waited for; matrix products, arithmetic and copies ran while one was open for 0% of the time, Pallas kernels for 0%

profile of v2, /device:TPU:1, one launch (start us, length us, event | category | flops | bytes accessed | tf_op | source)
XLA Modules:
  0.0 185.4 jit_solution(15876573620288161893)
XLA Ops:
  0.0 1.5 copy.33
  1.5 0.0 copy-start.5
  1.5 7.8 %all-to-all-start = ((bf16[16,8,256]{2,0,1:T(8,128)(2,1)}), bf16[16,8,256]{2,0,1:T(8,128)(2,1)S(1)}, u32[]{:S(2)}, u32[]{:S(2)}) async-start(bf16[16,8,256]{2,0,1:T(8,128)(2,1)} %bitcast.39), calls=%async_computation | async-start | bytes 131072 | tf_op jit(solution)/shard_map/all_to_all | solution.py:134
  9.3 0.0 copy-done.5
  9.3 0.1 eq.45
  9.4 0.2 convolution_convert_fusion.1
  9.6 0.0 copy-start.4
  9.6 0.2 fusion.5
  9.8 6.6 %all-to-all-done = bf16[16,8,256]{2,0,1:T(8,128)(2,1)S(1)} async-done(((bf16[16,8,256]{2,0,1:T(8,128)(2,1)}), bf16[16,8,256]{2,0,1:T(8,128)(2,1)S(1)}, u32[]{:S(2)}, u32[]{:S(2)}) %all-to-all-start) | async-done | bytes 65568 | tf_op jit(solution)/shard_map/all_to_all | solution.py:134
  16.5 0.0 copy-done.4
  16.5 0.0 copy-start.3
  16.5 1.1 convolution_convert_fusion
  17.6 15.4 %all-to-all-start.1 = ((bf16[64,16,256]{2,1,0:T(8,128)(2,1)}), bf16[64,16,256]{2,1,0:T(8,128)(2,1)S(1)}, u32[]{:S(2)}, u32[]{:S(2)}) async-start(bf16[64,16,256]{2,1,0:T(8,128)(2,1)} %bitcast.4), calls=%async_computation.1 | async-start | bytes 1048576 | tf_op jit(solution)/shard_map/all_to_all | solution.py:148
  33.0 0.0 copy-done.3
  33.1 0.2 copy.31
  33.2 0.1 copy.27
  33.4 0.0 copy-start
  33.4 0.0 copy-start.1
  33.4 17.3 %all-to-all-done.1 = bf16[64,16,256]{2,1,0:T(8,128)(2,1)S(1)} async-done(((bf16[64,16,256]{2,1,0:T(8,128)(2,1)}), bf16[64,16,256]{2,1,0:T(8,128)(2,1)S(1)}, u32[]{:S(2)}, u32[]{:S(2)}) %all-to-all-start.1) | async-done | bytes 524320 | tf_op jit(solution)/shard_map/all_to_all | solution.py:148
  50.7 24.5 %all_to_all.58 = bf16[176,8,256]{2,0,1:T(8,128)(2,1)S(1)} all-to-all(bf16[176,8,256]{2,0,1:T(8,128)(2,1)S(1)} %copy.27), channel_id=1, replica_groups=mesh['ep'=64,'tp'=8] {'tp'}, dimensions={1} | all-to-all | bytes 1441792 | tf_op jit(solution)/shard_map/all_to_all | solution.py:135
  75.3 0.0 copy-start.2
  75.3 0.0 copy-done
  75.3 0.0 copy-done.1
  75.3 0.7 copy-done.2
  76.0 72.0 %shard_map.82 = bf16[2,512,256]{2,1,0:T(8,128)(2,1)} custom-call(bf16[2,512,256]{2,1,0:T(8,128)(2,1)S(1)} %bitcast.41, bf16[176,2048]{1,0:T(8,128)(2,1)S(1)} %bitcast.42, bf16[176,2048]{1,0:T(8,128)(2,1)S(1)} %bitcast.43, bf16[8,176,256]{2,1,0:T(8,128)(2,1)S(1)} %bitcast.40, f32[1,2048]{1,0:T(1,128)S(1)} %bitcast.44), custom_call_target="tpu_custom_call" | custom-call | tf_op jit(solution)/shard_map/pallas_call | solution.py:109
  147.9 0.0 copy-start.6
  148.0 7.3 %all-to-all-start.3 = ((bf16[64,16,256]{2,1,0:T(8,128)(2,1)}), bf16[64,16,256]{2,1,0:T(8,128)(2,1)S(1)}, u32[]{:S(2)}, u32[]{:S(2)}) async-start(bf16[64,16,256]{2,1,0:T(8,128)(2,1)} %bitcast.10), calls=%async_computation.3 | async-start | bytes 1048576 | tf_op jit(solution)/shard_map/all_to_all | solution.py:157
  155.3 0.0 copy-done.6
  155.3 17.6 %all-to-all-done.3 = bf16[64,16,256]{2,1,0:T(8,128)(2,1)S(1)} async-done(((bf16[64,16,256]{2,1,0:T(8,128)(2,1)}), bf16[64,16,256]{2,1,0:T(8,128)(2,1)S(1)}, u32[]{:S(2)}, u32[]{:S(2)}) %all-to-all-start.3) | async-done | bytes 524320 | tf_op jit(solution)/shard_map/all_to_all | solution.py:157
  172.9 0.6 fusion.1
  173.6 11.2 %all_to_all.59 = bf16[8,16,256]{2,1,0:T(8,128)(2,1)S(1)} all-to-all(bf16[8,16,256]{2,1,0:T(8,128)(2,1)S(1)} %bitcast.49), channel_id=1, replica_groups=mesh['ep'=64,'tp'=8] {'tp'}, dimensions={0} | all-to-all | bytes 131072 | tf_op jit(solution)/shard_map/all_to_all | solution.py:160
  184.8 0.6 copy.30
  (6 shorter events, 0.1 us)
Async XLA Ops:
  1.5 7.8 %copy-start.5 = (s32[128,6]{0,1:T(8,128)S(1)}, s32[128,6]{0,1:T(8,128)}, u32[]{:S(2)}) copy-start(s32[128,6]{0,1:T(8,128)} %param.11) | copy-start | bytes 9220
  1.5 15.0 %all-to-all-start = ((bf16[16,8,256]{2,0,1:T(8,128)(2,1)}), bf16[16,8,256]{2,0,1:T(8,128)(2,1)S(1)}, u32[]{:S(2)}, u32[]{:S(2)}) async-start(bf16[16,8,256]{2,0,1:T(8,128)(2,1)} %bitcast.39), calls=%async_computation | async-start | bytes 131072 | tf_op jit(solution)/shard_map/all_to_all | solution.py:134
  9.6 6.9 %copy-start.4 = (bf16[128,256]{1,0:T(8,128)(2,1)S(1)}, bf16[128,256]{1,0:T(8,128)(2,1)}, u32[]{:S(2)}) copy-start(bf16[128,256]{1,0:T(8,128)(2,1)} %param.8) | copy-start | bytes 196612
  16.5 16.5 %copy-start.3 = (bf16[1,176,2048]{2,1,0:T(8,128)(2,1)S(1)}, bf16[1,176,2048]{2,1,0:T(8,128)(2,1)}, u32[]{:S(2)}) copy-start(bf16[1,176,2048]{2,1,0:T(8,128)(2,1)} %param.15) | copy-start | bytes 2162692
  17.6 33.1 %all-to-all-start.1 = ((bf16[64,16,256]{2,1,0:T(8,128)(2,1)}), bf16[64,16,256]{2,1,0:T(8,128)(2,1)S(1)}, u32[]{:S(2)}, u32[]{:S(2)}) async-start(bf16[64,16,256]{2,1,0:T(8,128)(2,1)} %bitcast.4), calls=%async_computation.1 | async-start | bytes 1048576 | tf_op jit(solution)/shard_map/all_to_all | solution.py:148
  33.4 41.9 %copy-start = (bf16[1,176,2048]{2,1,0:T(8,128)(2,1)S(1)}, bf16[1,176,2048]{2,1,0:T(8,128)(2,1)}, u32[]{:S(2)}) copy-start(bf16[1,176,2048]{2,1,0:T(8,128)(2,1)} %param.13) | copy-start | bytes 2162692
  33.4 41.9 %copy-start.1 = (bf16[1,176,2048]{2,1,0:T(8,128)(2,1)S(1)}, bf16[1,176,2048]{2,1,0:T(8,128)(2,1)}, u32[]{:S(2)}) copy-start(bf16[1,176,2048]{2,1,0:T(8,128)(2,1)} %param.14) | copy-start | bytes 2162692
  75.3 0.7 copy-start.2
  147.9 7.3 %copy-start.6 = (f32[128,6]{0,1:T(8,128)S(1)}, f32[128,6]{0,1:T(8,128)}, u32[]{:S(2)}) copy-start(f32[128,6]{0,1:T(8,128)} %param.12) | copy-start | bytes 9220
  148.0 25.0 %all-to-all-start.3 = ((bf16[64,16,256]{2,1,0:T(8,128)(2,1)}), bf16[64,16,256]{2,1,0:T(8,128)(2,1)S(1)}, u32[]{:S(2)}, u32[]{:S(2)}) async-start(bf16[64,16,256]{2,1,0:T(8,128)(2,1)} %bitcast.10), calls=%async_computation.3 | async-start | bytes 1048576 | tf_op jit(solution)/shard_map/all_to_all | solution.py:157

commit v3 on v1

v3 whole, which is shorter than its diff:
```python
import functools

import jax
import jax.numpy as jnp
from jax import lax
from jax.experimental import pallas as pl
from jax.experimental.pallas import tpu as pltpu
from jax.sharding import PartitionSpec as P

F32 = jnp.float32
BF16 = jnp.bfloat16
MESH = pl.DeviceIdType.MESH
NT = (((1,), (1,)), ((), ()))
TN = (((0,), (0,)), ((), ()))
GROUPS = 2


def expert_kernel(n_ep, n, send, w_gate, w_up, w_down, gain, back, got, down, scaled, rows, acts, own_act, result,
                  pre_acc, sq_acc, out_acc, local_sem, disp_send, disp_recv, down_send, down_recv, ret_send, ret_recv,
                  row_send, row_recv, act_send, act_recv):
    ep, me = lax.axis_index("ep"), lax.axis_index("tp")
    after, before = lax.rem(me + 1, n), lax.rem(me + n - 1, n)
    half = n // 2
    cap, width = send.shape[1:]
    hidden = w_gate.shape[0]
    per = n_ep // (2 * GROUPS)
    part = per * cap

    barrier = pltpu.get_barrier_semaphore()

    @pl.loop(1, n_ep)
    def _(i):
        pl.semaphore_signal(barrier, inc=1, device_id={"ep": lax.rem(ep + i, n_ep)}, device_id_type=MESH)

    for i in range(1, n):
        pl.semaphore_signal(barrier, inc=1, device_id={"tp": lax.rem(me + i, n)}, device_id_type=MESH)

    keep_rows = pltpu.make_async_copy(send.at[ep], got.at[0], local_sem.at[0])
    keep_rows.start()
    mine = pl.ds(pl.multiple_of(me * width, width), width)
    keep_down = pltpu.make_async_copy(w_down.at[:, mine], down.at[me], local_sem.at[1])
    keep_down.start()
    pl.semaphore_wait(barrier, n_ep - 1 + n - 1)

    def dispatch(i):
        to = lax.rem(ep + i, n_ep)
        return pltpu.make_async_remote_copy(
            src_ref=send.at[to], dst_ref=got.at[i], send_sem=disp_send.at[i], recv_sem=disp_recv.at[i],
            device_id={"ep": to}, device_id_type=MESH)

    def relay(i):
        to = lax.rem(me + i, n)
        columns = pl.ds(pl.multiple_of(to * width, width), width)
        return pltpu.make_async_remote_copy(
            src_ref=w_down.at[:, columns], dst_ref=down.at[me], send_sem=down_send.at[i], recv_sem=down_recv.at[i],
            device_id={"tp": to}, device_id_type=MESH)

    def give_back(p):
        return pltpu.make_async_remote_copy(
            src_ref=result.at[p], dst_ref=back.at[ep], send_sem=ret_send.at[p], recv_sem=ret_recv.at[p],
            device_id={"ep": lax.rem(ep + n_ep - p, n_ep)}, device_id_type=MESH)

    @pl.loop(1, n_ep)
    def _(i):
        dispatch(i).start()

    for i in range(1, n):
        relay(i).start()

    for s in range(n):
        columns = slice(s * width, (s + 1) * width)
        scale = gain[:, columns]
        scaled[s, :hidden] = (w_gate[:, columns].astype(F32) * scale).astype(BF16)
        scaled[s, hidden:] = (w_up[:, columns].astype(F32) * scale).astype(BF16)
    pre_acc[...] = jnp.zeros_like(pre_acc)
    sq_acc[...] = jnp.zeros_like(sq_acc)
    out_acc[...] = jnp.zeros_like(out_acc)
    ones = jnp.ones((8, width), BF16)

    def origin(way, hop):
        return lax.rem(me + n - hop, n) if way == 0 else lax.rem(me + hop, n)

    def travels(way, hop, c):
        return hop < half - 1 or (hop == half - 1 and c % 2 == way)

    class Ring:
        def __init__(self, first, buf, send_sem, recv_sem, use, group):
            self.first, self.buf, self.sems, self.use = first, buf, (send_sem, recv_sem), use
            a, b = 2 * group, 2 * group + 1
            self.pairs = [((0, a), (1, b)), ((0, b), (1, a))]

        def copy(self, way, hop, c):
            return pltpu.make_async_remote_copy(
                src_ref=self.first(c) if hop == 0 else self.buf.at[way, hop - 1, c],
                dst_ref=self.buf.at[way, hop, c],
                send_sem=self.sems[0].at[way, hop, c],
                recv_sem=self.sems[1].at[way, hop, c],
                device_id={"tp": after if way == 0 else before},
                device_id_type=MESH)

        def start(self):
            for pair in self.pairs:
                for way, c in pair:
                    if travels(way, 0, c):
                        self.copy(way, 0, c).start()

        def run(self, hook=None):
            for way, c in self.pairs[0]:
                self.use(self.first(c), me, c)
            if half == 1 and hook:
                hook()
            for hop in range(1, half + 1):
                for pair in self.pairs:
                    landed = [(way, c) for way, c in pair if travels(way, hop - 1, c)]
                    for way, c in landed:
                        self.copy(way, hop - 1, c).wait_recv()
                        if travels(way, hop, c):
                            self.copy(way, hop, c).start()
                    if hook and hop == half - 1 and pair is self.pairs[1]:
                        hook()
                    for way, c in landed:
                        self.use(self.buf.at[way, hop - 1, c], origin(way, hop), c)

        def drain(self):
            for hop in range(half):
                for pair in self.pairs:
                    for way, c in pair:
                        if travels(way, hop, c):
                            self.copy(way, hop, c).wait_send()

    def project(block, src, c):
        x = block[...].reshape(part, width)
        pre_acc[c] += lax.dot_general(scaled[src], x, NT, preferred_element_type=F32)
        sq = x.astype(F32) * x.astype(F32)
        top = sq.astype(BF16)
        rest = (sq - top.astype(F32)).astype(BF16)
        sq_acc[c] += lax.dot_general(ones, top, NT, preferred_element_type=F32) + lax.dot_general(
            ones, rest, NT, preferred_element_type=F32)

    def reduce(block, src, c):
        out_acc[c] += lax.dot_general(block[...], down[src], TN, preferred_element_type=F32)

    def activate(group):
        for c in (2 * group, 2 * group + 1):
            r = lax.rsqrt(sq_acc[c][:1] / (n * width) + 1e-05)
            g = pre_acc[c][:hidden] * r
            own_act[c] = (g / (1.0 + jnp.exp(-g)) * (pre_acc[c][hidden:] * r)).astype(BF16)

    def arrive(group):
        @pl.loop(max(1, 2 * per * group), 2 * per * (group + 1))
        def _(i):
            dispatch(i).wait_recv()

    row_rings = [Ring(lambda c: got.at[pl.ds(c * per, per)], rows, row_send, row_recv, project, g) for g in range(GROUPS)]
    act_rings = [Ring(lambda c: own_act.at[c], acts, act_send, act_recv, reduce, g) for g in range(GROUPS)]

    def begin_rows(group):
        arrive(group)
        row_rings[group].start()

    keep_rows.wait()
    begin_rows(0)
    for g in range(GROUPS):
        if g + 1 < GROUPS:
            row_rings[g].run(functools.partial(begin_rows, g + 1))
        else:
            row_rings[g].run(act_rings[0].start)
        activate(g)
    keep_down.wait()
    for i in range(1, n):
        relay(i).wait_recv()
    keep_result = pltpu.make_async_copy(result.at[0], back.at[ep], local_sem.at[2])
    for g in range(GROUPS):
        act_rings[g].run(act_rings[g + 1].start if g + 1 < GROUPS else None)
        for c in (2 * g, 2 * g + 1):
            result[c * per:(c + 1) * per] = out_acc[c].astype(BF16).reshape(per, cap, width)
        if g == 0:
            keep_result.start()

        @pl.loop(max(1, 2 * per * g), 2 * per * (g + 1))
        def _(p):
            give_back(p).start()

    for ring in row_rings + act_rings:
        ring.drain()
    for i in range(1, n):
        relay(i).wait_send()
    keep_result.wait()

    @pl.loop(1, n_ep)
    def _(i):
        dispatch(i).wait_send()
        give_back(i).wait_send()
        give_back(i).wait_recv()


def experts(n_ep, n, send, w_gate, w_up, w_down, gain):
    _, cap, width = send.shape
    hidden = w_gate.shape[0]
    half = n // 2
    chunks = 2 * GROUPS
    per = n_ep // chunks
    part = per * cap
    vmem = pl.BlockSpec(memory_space=pltpu.VMEM)
    dma = pltpu.SemaphoreType.DMA
    ring = dma((2, half, chunks))
    return pl.pallas_call(
        functools.partial(expert_kernel, n_ep, n),
        out_shape=jax.ShapeDtypeStruct(send.shape, BF16),
        in_specs=[vmem] * 5,
        out_specs=vmem,
        scratch_shapes=[
            pltpu.VMEM(send.shape, BF16),
            pltpu.VMEM((n, hidden, width), BF16),
            pltpu.VMEM((n, 2 * hidden, width), BF16),
            pltpu.VMEM((2, half, chunks, per, cap, width), BF16),
            pltpu.VMEM((2, half, chunks, hidden, part), BF16),
            pltpu.VMEM((chunks, hidden, part), BF16),
            pltpu.VMEM(send.shape, BF16),
            pltpu.VMEM((chunks, 2 * hidden, part), F32),
            pltpu.VMEM((chunks, 8, part), F32),
            pltpu.VMEM((chunks, part, width), F32),
            dma((3,)), dma((n_ep,)), dma((n_ep,)), dma((n,)), dma((n,)), dma((n_ep,)), dma((n_ep,)),
            ring, ring, ring, ring,
        ],
        compiler_params=pltpu.CompilerParams(collective_id=0, has_side_effects=True, vmem_limit_bytes=48 * 2**20),
    )(send, w_gate, w_up, w_down, gain)


def per_device(attn_out, resid, norm_gain, expert_ids, gate_vals, w_gate, w_up, w_down):
    ep_count = lax.axis_size("ep")
    tp_count = lax.axis_size("tp")
    tok, top = expert_ids.shape
    cap = 4 * tok * top // (3 * ep_count)
    slots = ep_count * cap
    resid_cols = lax.all_to_all(resid, "tp", split_axis=1, concat_axis=0, tiled=True)
    h = (resid_cols.astype(F32) + attn_out.astype(F32)).astype(BF16)
    hit = expert_ids[:, :, None] == jnp.arange(ep_count, dtype=jnp.int32)[None, None, :]
    chosen = jnp.any(hit, axis=1).astype(BF16)
    gates = jnp.sum(jnp.where(hit, gate_vals[:, :, None], 0.0), axis=1)
    earlier = jnp.tril(jnp.ones((tok, tok), BF16), -1)
    rank = jnp.dot(earlier, chosen, preferred_element_type=F32).astype(jnp.int32)
    place = (chosen[:, :, None] > 0) & (
        rank[:, :, None] == jnp.arange(cap, dtype=jnp.int32)[None, None, :]
    )
    weights = jnp.where(place, gates[:, :, None], 0.0).reshape(tok, slots)
    place = place.astype(BF16).reshape(tok, slots)
    send = lax.dot_general(place, h, (((0,), (0,)), ((), ())), preferred_element_type=F32).astype(BF16)
    back = experts(
        ep_count, tp_count, send.reshape(ep_count, cap, -1), w_gate[0], w_up[0], w_down[0], norm_gain[None, :]
    )
    moe = jnp.dot(weights, back.reshape(slots, -1).astype(F32), precision=lax.Precision.HIGHEST)
    layer = (h.astype(F32) + moe).astype(BF16)
    return lax.all_to_all(layer, "tp", split_axis=0, concat_axis=1, tiled=True)


def solution(mesh):
    in_specs = (
        P("ep", "tp"),
        P(("ep", "tp"), None),
        P(),
        P("ep", None),
        P("ep", None),
        P("ep", "tp", None),
        P("ep", "tp", None),
        P("ep", "tp", None),
    )
    return jax.shard_map(
        per_device, mesh=mesh, in_specs=in_specs, out_specs=P(("ep", "tp"), None), check_vma=False
    )
```

time: 220 us -> 148 us (0.67)
  Pallas kernels: 0 us -> 116 us
  waiting for transfers between devices: 108 us -> 6.59 us
  blocking collectives: 63.2 us -> 11 us
  between operations: 13.6 us -> 0.11 us
  starting transfers between devices: 18.4 us -> 7.77 us
  matrix products: 9 us -> 1.11 us
  other arithmetic: 5.07 us -> 0.29 us
    pallas_call x0 -> x1, Pallas kernels: none -> 116 us  [experts(): pl.pallas_call(functools.partial(expert_kernel, n_ep, n), out_shape=jax.S...]
    all_gather x2 -> x0, waiting for transfers between devices: 84 us -> none  [the longest x1 52.2 us: per_device(): rows = lax.all_gather(got.reshape(slots, -1), 'tp', axis=1, tiled=True)]
    all_to_all x2 -> x0, blocking collectives: 52.1 us -> none  [the longest x1 33 us: per_device(): lax.all_to_all(send.reshape(ep_count, cap, -1), 'ep', split_axis=0, conca...]
    all_to_all x1 -> x0, waiting for transfers between devices: 17.6 us -> none  [per_device(): lax.all_to_all(out.reshape(ep_count, cap, -1), 'ep', split_axis=0, concat...]
    all_to_all x1 -> x0, starting transfers between devices: 10.7 us -> none  [per_device(): lax.all_to_all(out.reshape(ep_count, cap, -1), 'ep', split_axis=0, concat...]
    dot_general x3 -> x0, matrix products: 7.89 us -> none  [the longest x1 3.65 us: per_device(): lax.dot_general(act_all, down_cols, (((0,), (0,)), ((), ())), preferred_e...]
    reduce_sum x1 -> x0, other arithmetic: 3.22 us -> none  [per_device(): mean_sq = jnp.mean(rows_f * rows_f, axis=-1, keepdims=True)]
  transfers between devices with their start and end apart: 4 -> 1, of which waited for: 4 -> 1; matrix products, arithmetic and copies ran while one was open for 1% -> 0% of each run, Pallas kernels for 0% -> 0%
where the time goes in v3:
time: 148 us; the launch traced here: 147 us
  Pallas kernels  116 us (78%)
  blocking collectives  11 us (7%)
  starting transfers between devices  7.77 us (5%)
  waiting for transfers between devices  6.59 us (4%)
  local copies, waits for them, and re-layouts  4.04 us (3%)
    pallas_call x1, Pallas kernels, experts(): pl.pallas_call(functools.partial(expert_kernel, n_ep, n), out_shape=jax.S...  116 us
    all_to_all x1, blocking collectives, per_device(): return lax.all_to_all(layer, 'tp', split_axis=0, concat_axis=1, tiled=True)  11 us
    all_to_all x1, starting transfers between devices, per_device(): lax.all_to_all(resid, 'tp', split_axis=1, concat_axis=0, tiled=True)  7.77 us
    all_to_all x1, waiting for transfers between devices, per_device(): lax.all_to_all(resid, 'tp', split_axis=1, concat_axis=0, tiled=True)  6.59 us
  transfers between devices with their start and end apart: 1, of which 1 were waited for; matrix products, arithmetic and copies ran while one was open for 0% of the time, Pallas kernels for 0%

profile of v3, /device:TPU:1, one launch (start us, length us, event | category | flops | bytes accessed | tf_op | source)
XLA Modules:
  0.0 147.3 jit_solution(1173372870624871480)
XLA Ops:
  0.0 0.0 copy-start.5
  0.0 0.0 copy-start.6
  0.0 0.0 copy-start.4
  0.0 1.5 %copy.25 = bf16[2,8,8,256]{3,2,0,1:T(8,128)(2,1)} copy(bf16[2,8,8,256]{3,2,1,0:T(8,128)(2,1)} %bitcast.41) | data formatting | bytes 131072 | tf_op jit(solution)/shard_map/all_to_all | solution.py:236
  1.5 0.0 copy-start
  1.5 0.0 copy-start.1
  1.5 7.8 %all-to-all-start = ((bf16[16,8,256]{2,0,1:T(8,128)(2,1)}), bf16[16,8,256]{2,0,1:T(8,128)(2,1)S(1)}, u32[]{:S(2)}, u32[]{:S(2)}) async-start(bf16[16,8,256]{2,0,1:T(8,128)(2,1)} %bitcast.34), calls=%async_computation | async-start | bytes 131072 | tf_op jit(solution)/shard_map/all_to_all | solution.py:236
  9.3 0.0 copy-done.5
  9.4 0.2 convolution_convert_fusion.1
  9.6 0.1 eq.45
  9.7 0.2 fusion.5
  9.9 0.0 copy-done.6
  9.9 6.6 %all-to-all-done = bf16[16,8,256]{2,0,1:T(8,128)(2,1)S(1)} async-done(((bf16[16,8,256]{2,0,1:T(8,128)(2,1)}), bf16[16,8,256]{2,0,1:T(8,128)(2,1)S(1)}, u32[]{:S(2)}, u32[]{:S(2)}) %all-to-all-start) | async-done | bytes 65568 | tf_op jit(solution)/shard_map/all_to_all | solution.py:236
  16.5 0.0 copy-done.4
  16.5 0.3 convolution_convert_fusion
  16.9 0.0 copy-start.3
  16.9 0.0 copy-done
  16.9 0.0 copy-done.1
  16.9 0.7 copy-done.3
  17.6 0.0 copy-start.2
  17.6 1.1 copy-done.2
  18.7 116.4 %shard_map.82 = bf16[64,16,256]{2,1,0:T(8,128)(2,1)S(1)} custom-call(bf16[64,16,256]{2,1,0:T(8,128)(2,1)S(1)} %bitcast.35, bf16[176,2048]{1,0:T(8,128)(2,1)S(1)} %bitcast.36, bf16[176,2048]{1,0:T(8,128)(2,1)S(1)} %bitcast.37, bf16[176,2048]{1,0:T(8,128)(2,1)S(1)} %bitcast.38, f32[1,2048]{1,0:T(1,128)S(1)} %bitcast.39), custom_call_target="tpu_custom_call" | custom-call | tf_op jit(solution)/shard_map/pallas_call | solution.py:207
  135.0 0.6 fusion.1
  135.7 11.0 %all_to_all.32 = bf16[8,16,256]{2,1,0:T(8,128)(2,1)S(1)} all-to-all(bf16[8,16,256]{2,1,0:T(8,128)(2,1)S(1)} %bitcast.42), channel_id=1, replica_groups=mesh['ep'=64,'tp'=8] {'tp'}, dimensions={0} | all-to-all | bytes 131072 | tf_op jit(solution)/shard_map/all_to_all | solution.py:254
  146.7 0.6 copy.23
  (6 shorter events, 0.1 us)
Async XLA Ops:
  0.0 9.3 %copy-start.5 = (s32[128,6]{0,1:T(8,128)S(1)}, s32[128,6]{0,1:T(8,128)}, u32[]{:S(2)}) copy-start(s32[128,6]{0,1:T(8,128)} %param.11) | copy-start | bytes 9220
  0.0 9.9 %copy-start.6 = (f32[128,6]{0,1:T(8,128)S(1)}, f32[128,6]{0,1:T(8,128)}, u32[]{:S(2)}) copy-start(f32[128,6]{0,1:T(8,128)} %param.12) | copy-start | bytes 9220
  0.0 16.5 %copy-start.4 = (bf16[128,256]{1,0:T(8,128)(2,1)S(1)}, bf16[128,256]{1,0:T(8,128)(2,1)}, u32[]{:S(2)}) copy-start(bf16[128,256]{1,0:T(8,128)(2,1)} %param.8) | copy-start | bytes 196612
  1.5 15.3 %copy-start = (bf16[1,176,2048]{2,1,0:T(8,128)(2,1)S(1)}, bf16[1,176,2048]{2,1,0:T(8,128)(2,1)}, u32[]{:S(2)}) copy-start(bf16[1,176,2048]{2,1,0:T(8,128)(2,1)} %param.13) | copy-start | bytes 2162692
  1.5 15.4 %copy-start.1 = (bf16[1,176,2048]{2,1,0:T(8,128)(2,1)S(1)}, bf16[1,176,2048]{2,1,0:T(8,128)(2,1)}, u32[]{:S(2)}) copy-start(bf16[1,176,2048]{2,1,0:T(8,128)(2,1)} %param.14) | copy-start | bytes 2162692
  1.5 15.0 %all-to-all-start = ((bf16[16,8,256]{2,0,1:T(8,128)(2,1)}), bf16[16,8,256]{2,0,1:T(8,128)(2,1)S(1)}, u32[]{:S(2)}, u32[]{:S(2)}) async-start(bf16[16,8,256]{2,0,1:T(8,128)(2,1)} %bitcast.34), calls=%async_computation | async-start | bytes 131072 | tf_op jit(solution)/shard_map/all_to_all | solution.py:236
  16.9 0.7 copy-start.3
  17.6 1.1 copy-start.2

commit v4 on v3

--- a/solution.py
+++ b/solution.py
@@ -15,13 +15,16 @@
 GROUPS = 2
 
 
-def expert_kernel(n_ep, n, send, w_gate, w_up, w_down, gain, back, got, down, scaled, rows, acts, own_act, result,
-                  pre_acc, sq_acc, out_acc, local_sem, disp_send, disp_recv, down_send, down_recv, ret_send, ret_recv,
-                  row_send, row_recv, act_send, act_recv):
+def layer_kernel(n_ep, n, cap, attn, resid, gain, ids, gates, w_gate, w_up, w_down, out, own_resid, h_buf, place, weights,
+                 raw, send, got, down, scaled, rows, acts, own_act, result, back, pre_acc, sq_acc, out_acc, layer,
+                 local_sem, res_send, res_recv, fin_send, fin_recv, disp_send, disp_recv, down_send, down_recv,
+                 ret_send, ret_recv, row_send, row_recv, act_send, act_recv):
     ep, me = lax.axis_index("ep"), lax.axis_index("tp")
     after, before = lax.rem(me + 1, n), lax.rem(me + n - 1, n)
     half = n // 2
-    cap, width = send.shape[1:]
+    tok, width = attn.shape
+    top = ids.shape[1]
+    slots = n_ep * cap
     hidden = w_gate.shape[0]
     per = n_ep // (2 * GROUPS)
     part = per * cap
@@ -35,17 +38,60 @@
     for i in range(1, n):
         pl.semaphore_signal(barrier, inc=1, device_id={"tp": lax.rem(me + i, n)}, device_id_type=MESH)
 
-    keep_rows = pltpu.make_async_copy(send.at[ep], got.at[0], local_sem.at[0])
-    keep_rows.start()
     mine = pl.ds(pl.multiple_of(me * width, width), width)
+    keep_resid = pltpu.make_async_copy(resid.at[:, mine], own_resid.at[me], local_sem.at[0])
     keep_down = pltpu.make_async_copy(w_down.at[:, mine], down.at[me], local_sem.at[1])
-    keep_down.start()
+    load_gate = pltpu.make_async_copy(w_gate, raw.at[0], local_sem.at[2])
+    load_up = pltpu.make_async_copy(w_up, raw.at[1], local_sem.at[3])
+    for load in (keep_resid, load_gate, load_up, keep_down):
+        load.start()
+
+    def iota(shape, dim):
+        return lax.broadcasted_iota(jnp.int32, shape, dim)
+
+    ahead = iota((n_ep, slots), 0) - ep
+    low = jnp.where(ahead < 0, ahead + n_ep, ahead) * cap
+    slot = iota((n_ep, slots), 1)
+    inside = (slot >= low) & (slot < low + cap)
+    spread = jnp.where(inside, 1.0, 0.0).astype(BF16)
+    nth = slot[:1].astype(F32) - jnp.sum(jnp.where(inside, low.astype(F32), 0.0), axis=0, keepdims=True)
+    chosen = jnp.zeros((tok, n_ep), F32)
+    gate = jnp.zeros((tok, n_ep), F32)
+    for k in range(top):
+        hit = ids[:, k:k + 1] == iota((tok, n_ep), 1)
+        chosen += jnp.where(hit, 1.0, 0.0)
+        gate += jnp.where(hit, gates[:, k:k + 1], 0.0)
+    earlier = jnp.where(iota((tok, tok), 0) > iota((tok, tok), 1), 1.0, 0.0).astype(BF16)
+    rank = jnp.dot(earlier, chosen.astype(BF16), preferred_element_type=F32)
+    spot = jnp.where(chosen > 0, rank, float(tok)).astype(BF16)
+    taken = jnp.dot(spot, spread, preferred_element_type=F32) == nth
+    place[...] = jnp.where(taken, 1.0, 0.0).astype(BF16)
+    rest = gate
+    for term in range(3):
+        piece = rest.astype(BF16)
+        rest = rest - piece.astype(F32)
+        wide = jnp.dot(piece, spread, preferred_element_type=F32)
+        weights[term] = jnp.where(taken, wide, 0.0).astype(BF16)
+
     pl.semaphore_wait(barrier, n_ep - 1 + n - 1)
+
+    def to_columns(i):
+        to = lax.rem(me + i, n)
+        columns = pl.ds(pl.multiple_of(to * width, width), width)
+        return pltpu.make_async_remote_copy(
+            src_ref=resid.at[:, columns], dst_ref=own_resid.at[me], send_sem=res_send.at[i], recv_sem=res_recv.at[i],
+            device_id={"tp": to}, device_id_type=MESH)
+
+    def to_rows(i):
+        to = lax.rem(me + i, n)
+        return pltpu.make_async_remote_copy(
+            src_ref=layer.at[to], dst_ref=out.at[:, mine], send_sem=fin_send.at[i], recv_sem=fin_recv.at[i],
+            device_id={"tp": to}, device_id_type=MESH)
 
     def dispatch(i):
         to = lax.rem(ep + i, n_ep)
         return pltpu.make_async_remote_copy(
-            src_ref=send.at[to], dst_ref=got.at[i], send_sem=disp_send.at[i], recv_sem=disp_recv.at[i],
+            src_ref=send.at[i], dst_ref=got.at[i], send_sem=disp_send.at[i], recv_sem=disp_recv.at[i],
             device_id={"ep": to}, device_id_type=MESH)
 
     def relay(i):
@@ -57,21 +103,39 @@
 
     def give_back(p):
         return pltpu.make_async_remote_copy(
-            src_ref=result.at[p], dst_ref=back.at[ep], send_sem=ret_send.at[p], recv_sem=ret_recv.at[p],
+            src_ref=result.at[p], dst_ref=back.at[p], send_sem=ret_send.at[p], recv_sem=ret_recv.at[p],
             device_id={"ep": lax.rem(ep + n_ep - p, n_ep)}, device_id_type=MESH)
 
-    @pl.loop(1, n_ep)
-    def _(i):
-        dispatch(i).start()
-
+    def blocks(group):
+        return slice(2 * per * group, 2 * per * (group + 1))
+
+    for i in range(1, n):
+        to_columns(i).start()
     for i in range(1, n):
         relay(i).start()
-
+    keep_resid.wait()
+    for i in range(1, n):
+        to_columns(i).wait_recv()
+    h = (own_resid[...].reshape(tok, width).astype(F32) + attn[...].astype(F32)).astype(BF16)
+    h_buf[...] = h
+    keep_rows = pltpu.make_async_copy(send.at[0], got.at[0], local_sem.at[4])
+    for g in range(GROUPS):
+        x = lax.dot_general(place[:, 2 * part * g:2 * part * (g + 1)], h, TN, preferred_element_type=F32)
+        send[blocks(g)] = x.astype(BF16).reshape(2 * per, cap, width)
+        if g == 0:
+            keep_rows.start()
+
+        @pl.loop(max(1, 2 * per * g), 2 * per * (g + 1))
+        def _(i):
+            dispatch(i).start()
+
+    load_gate.wait()
+    load_up.wait()
     for s in range(n):
         columns = slice(s * width, (s + 1) * width)
         scale = gain[:, columns]
-        scaled[s, :hidden] = (w_gate[:, columns].astype(F32) * scale).astype(BF16)
-        scaled[s, hidden:] = (w_up[:, columns].astype(F32) * scale).astype(BF16)
+        scaled[s, :hidden] = (raw[0, :, columns].astype(F32) * scale).astype(BF16)
+        scaled[s, hidden:] = (raw[1, :, columns].astype(F32) * scale).astype(BF16)
     pre_acc[...] = jnp.zeros_like(pre_acc)
     sq_acc[...] = jnp.zeros_like(sq_acc)
     out_acc[...] = jnp.zeros_like(out_acc)
@@ -169,7 +233,7 @@
     keep_down.wait()
     for i in range(1, n):
         relay(i).wait_recv()
-    keep_result = pltpu.make_async_copy(result.at[0], back.at[ep], local_sem.at[2])
+    keep_result = pltpu.make_async_copy(result.at[0], back.at[0], local_sem.at[5])
     for g in range(GROUPS):
         act_rings[g].run(act_rings[g + 1].start if g + 1 < GROUPS else None)
         for c in (2 * g, 2 * g + 1):
@@ -181,77 +245,83 @@
         def _(p):
             give_back(p).start()
 
+    moe = jnp.zeros((tok, width), F32)
+    for g in range(GROUPS):
+        if g == 0:
+            keep_result.wait()
+
+        @pl.loop(max(1, 2 * per * g), 2 * per * (g + 1))
+        def _(p):
+            give_back(p).wait_recv()
+
+        x = back[blocks(g)].reshape(2 * part, width)
+        for term in range(3):
+            moe += jnp.dot(weights[term, :, 2 * part * g:2 * part * (g + 1)], x, preferred_element_type=F32)
+    layer[...] = (h_buf[...].astype(F32) + moe).astype(BF16).reshape(layer.shape)
+    keep_layer = pltpu.make_async_copy(layer.at[me], out.at[:, mine], local_sem.at[6])
+    keep_layer.start()
+    for i in range(1, n):
+        to_rows(i).start()
+
     for ring in row_rings + act_rings:
         ring.drain()
     for i in range(1, n):
         relay(i).wait_send()
-    keep_result.wait()
+        to_columns(i).wait_send()
 
     @pl.loop(1, n_ep)
     def _(i):
         dispatch(i).wait_send()
         give_back(i).wait_send()
-        give_back(i).wait_recv()
-
-
-def experts(n_ep, n, send, w_gate, w_up, w_down, gain):
-    _, cap, width = send.shape
-    hidden = w_gate.shape[0]
+
+    keep_layer.wait()
+    for i in range(1, n):
+        to_rows(i).wait_send()
+        to_rows(i).wait_recv()
+
+
+def per_device(attn_out, resid, norm_gain, expert_ids, gate_vals, w_gate, w_up, w_down):
+    n_ep, n = lax.axis_size("ep"), lax.axis_size("tp")
+    tok, width = attn_out.shape
+    hidden = w_gate.shape[1]
+    cap = 4 * tok * expert_ids.shape[1] // (3 * n_ep)
     half = n // 2
     chunks = 2 * GROUPS
     per = n_ep // chunks
     part = per * cap
-    vmem = pl.BlockSpec(memory_space=pltpu.VMEM)
+    vmem, anywhere = pl.BlockSpec(memory_space=pltpu.VMEM), pl.BlockSpec(memory_space=pl.ANY)
     dma = pltpu.SemaphoreType.DMA
     ring = dma((2, half, chunks))
+    block = (n_ep, cap, width)
     return pl.pallas_call(
-        functools.partial(expert_kernel, n_ep, n),
-        out_shape=jax.ShapeDtypeStruct(send.shape, BF16),
-        in_specs=[vmem] * 5,
+        functools.partial(layer_kernel, n_ep, n, cap),
+        out_shape=jax.ShapeDtypeStruct(resid.shape, BF16),
+        in_specs=[vmem] * 5 + [anywhere] * 3,
         out_specs=vmem,
         scratch_shapes=[
-            pltpu.VMEM(send.shape, BF16),
+            pltpu.VMEM((n, tok // n, width), BF16),
+            pltpu.VMEM((tok, width), BF16),
+            pltpu.VMEM((tok, n_ep * cap), BF16),
+            pltpu.VMEM((3, tok, n_ep * cap), BF16),
+            pltpu.VMEM((2, hidden, n * width), BF16),
+            pltpu.VMEM(block, BF16),
+            pltpu.VMEM(block, BF16),
             pltpu.VMEM((n, hidden, width), BF16),
             pltpu.VMEM((n, 2 * hidden, width), BF16),
             pltpu.VMEM((2, half, chunks, per, cap, width), BF16),
             pltpu.VMEM((2, half, chunks, hidden, part), BF16),
             pltpu.VMEM((chunks, hidden, part), BF16),
-            pltpu.VMEM(send.shape, BF16),
+            pltpu.VMEM(block, BF16),
+            pltpu.VMEM(block, BF16),
             pltpu.VMEM((chunks, 2 * hidden, part), F32),
             pltpu.VMEM((chunks, 8, part), F32),
             pltpu.VMEM((chunks, part, width), F32),
-            dma((3,)), dma((n_ep,)), dma((n_ep,)), dma((n,)), dma((n,)), dma((n_ep,)), dma((n_ep,)),
-            ring, ring, ring, ring,
+            pltpu.VMEM((n, tok // n, width), BF16),
+            dma((7,)), dma((n,)), dma((n,)), dma((n,)), dma((n,)), dma((n_ep,)), dma((n_ep,)), dma((n,)), dma((n,)),
+            dma((n_ep,)), dma((n_ep,)), ring, ring, ring, ring,
         ],
         compiler_params=pltpu.CompilerParams(collective_id=0, has_side_effects=True, vmem_limit_bytes=48 * 2**20),
-    )(send, w_gate, w_up, w_down, gain)
-
-
-def per_device(attn_out, resid, norm_gain, expert_ids, gate_vals, w_gate, w_up, w_down):
-    ep_count = lax.axis_size("ep")
-    tp_count = lax.axis_size("tp")
-    tok, top = expert_ids.shape
-    cap = 4 * tok * top // (3 * ep_count)
-    slots = ep_count * cap
-    resid_cols = lax.all_to_all(resid, "tp", split_axis=1, concat_axis=0, tiled=True)
-    h = (resid_cols.astype(F32) + attn_out.astype(F32)).astype(BF16)
-    hit = expert_ids[:, :, None] == jnp.arange(ep_count, dtype=jnp.int32)[None, None, :]
-    chosen = jnp.any(hit, axis=1).astype(BF16)
-    gates = jnp.sum(jnp.where(hit, gate_vals[:, :, None], 0.0), axis=1)
-    earlier = jnp.tril(jnp.ones((tok, tok), BF16), -1)
-    rank = jnp.dot(earlier, chosen, preferred_element_type=F32).astype(jnp.int32)
-    place = (chosen[:, :, None] > 0) & (
-        rank[:, :, None] == jnp.arange(cap, dtype=jnp.int32)[None, None, :]
-    )
-    weights = jnp.where(place, gates[:, :, None], 0.0).reshape(tok, slots)
-    place = place.astype(BF16).reshape(tok, slots)
-    send = lax.dot_general(place, h, (((0,), (0,)), ((), ())), preferred_element_type=F32).astype(BF16)
-    back = experts(
-        ep_count, tp_count, send.reshape(ep_count, cap, -1), w_gate[0], w_up[0], w_down[0], norm_gain[None, :]
-    )
-    moe = jnp.dot(weights, back.reshape(slots, -1).astype(F32), precision=lax.Precision.HIGHEST)
-    layer = (h.astype(F32) + moe).astype(BF16)
-    return lax.all_to_all(layer, "tp", split_axis=0, concat_axis=1, tiled=True)
+    )(attn_out, resid, norm_gain[None, :], expert_ids, gate_vals, w_gate[0], w_up[0], w_down[0])
 
 
 def solution(mesh):

time: 148 us -> 134 us (0.905)
  Pallas kernels: 116 us -> 128 us
  blocking collectives: 11 us -> 0 us
  starting transfers between devices: 7.77 us -> 0 us
  waiting for transfers between devices: 6.59 us -> 0 us
  local copies, waits for them, and re-layouts: 4.04 us -> 5.57 us
    pallas_call x1, Pallas kernels: 116 us -> 128 us  [per_device(): pl.pallas_call(functools.partial(layer_kernel, n_ep, n, cap), out_shape=j...]
    all_to_all x1 -> x0, blocking collectives: 11 us -> none  [per_device(): return lax.all_to_all(layer, 'tp', split_axis=0, concat_axis=1, tiled=True)]
    all_to_all x1 -> x0, starting transfers between devices: 7.77 us -> none  [per_device(): lax.all_to_all(resid, 'tp', split_axis=1, concat_axis=0, tiled=True)]
    all_to_all x1 -> x0, waiting for transfers between devices: 6.59 us -> none  [per_device(): lax.all_to_all(resid, 'tp', split_axis=1, concat_axis=0, tiled=True)]
    unnamed x14 -> x17, local copies, waits for them, and re-layouts: 1.8 us -> 5.57 us
    all_to_all x2 -> x0, local copies, waits for them, and re-layouts: 2.14 us -> none  [the longest x1 1.51 us: per_device(): lax.all_to_all(resid, 'tp', split_axis=1, concat_axis=0, tiled=True)]
  transfers between devices with their start and end apart: 1 -> 0, of which waited for: 1 -> 0; matrix products, arithmetic and copies ran while one was open for 0% -> 0% of each run, Pallas kernels for 0% -> 0%
where the time goes in v4:
time: 134 us; the launch traced here: 133 us
  Pallas kernels  128 us (96%)
  local copies, waits for them, and re-layouts  5.57 us (4%)
    pallas_call x1, Pallas kernels, per_device(): pl.pallas_call(functools.partial(layer_kernel, n_ep, n, cap), out_shape=j...  128 us
    unnamed x17, local copies, waits for them, and re-layouts  5.57 us

profile of v4, /device:TPU:1, one launch (start us, length us, event | category | flops | bytes accessed | tf_op | source)
XLA Modules:
  0.0 133.2 jit_solution(1117076433664457361)
XLA Ops:
  0.0 0.0 copy-start.6
  0.0 0.7 copy-done.6
  0.7 0.0 copy-start.3
  0.7 0.0 copy-start.4
  0.7 0.1 copy.9.ids
  0.8 0.0 copy-start.5
  0.8 0.8 copy.10.gates
  1.6 0.0 copy-done.3
  1.6 0.0 copy-done.4
  1.6 0.0 copy-done.5
  1.6 0.0 copy-start
  1.6 1.1 copy-done
  2.8 0.0 copy-start.1
  2.8 1.1 copy-done.1
  3.9 0.0 copy-start.2
  3.9 1.1 copy-done.2
  5.0 127.6 %shard_map.82 = bf16[16,2048]{1,0:T(8,128)(2,1)S(1)} custom-call(bf16[128,256]{1,0:T(8,128)(2,1)S(1)} %copy-done.3, bf16[16,2048]{1,0:T(8,128)(2,1)S(1)} %copy-done.4, f32[1,2048]{1,0:T(1,128)S(1)} %bitcast.7, s32[128,6]{1,0:T(8,128)S(1)} %copy.9.ids, f32[128,6]{1,0:T(8,128)S(1)} %copy.10.gates, bf16[176,2048]{1,0:T(8,128)(2,1)S(1)} %bitcast.4, ...), custom_call_target="tpu_custom_call" | custom-call | tf_op jit(solution)/shard_map/pallas_call | solution.py:296
  132.6 0.6 copy.12
Async XLA Ops:
  0.0 0.7 copy-start.6
  0.7 0.9 copy-start.3
  0.7 0.9 copy-start.4
  0.8 0.8 copy-start.5
  1.6 1.1 copy-start
  2.8 1.1 copy-start.1
  3.9 1.1 copy-start.2

commit v5 on v4

--- a/solution.py
+++ b/solution.py
@@ -17,7 +17,7 @@
 
 def layer_kernel(n_ep, n, cap, attn, resid, gain, ids, gates, w_gate, w_up, w_down, out, own_resid, h_buf, place, weights,
                  raw, send, got, down, scaled, rows, acts, own_act, result, back, pre_acc, sq_acc, out_acc, layer,
-                 local_sem, res_send, res_recv, fin_send, fin_recv, disp_send, disp_recv, down_send, down_recv,
+                 row_sem, local_sem, res_send, res_recv, fin_send, fin_recv, disp_send, disp_recv, down_send, down_recv,
                  ret_send, ret_recv, row_send, row_recv, act_send, act_recv):
     ep, me = lax.axis_index("ep"), lax.axis_index("tp")
     after, before = lax.rem(me + 1, n), lax.rem(me + n - 1, n)
@@ -31,10 +31,14 @@
 
     barrier = pltpu.get_barrier_semaphore()
 
-    @pl.loop(1, n_ep)
-    def _(i):
-        pl.semaphore_signal(barrier, inc=1, device_id={"ep": lax.rem(ep + i, n_ep)}, device_id_type=MESH)
-
+    count = max(1, n_ep // 4)
+    row, place_in_row = lax.div(ep, count), lax.rem(ep, count)
+    for i in range(1, count):
+        pl.semaphore_signal(
+            barrier, inc=1, device_id={"ep": row * count + lax.rem(place_in_row + i, count)}, device_id_type=MESH)
+    column = [lax.rem(ep + i * count, n_ep) for i in range(1, n_ep // count)]
+    for peer in column:
+        pl.semaphore_signal(barrier, inc=1, device_id={"ep": peer}, device_id_type=MESH)
     for i in range(1, n):
         pl.semaphore_signal(barrier, inc=1, device_id={"tp": lax.rem(me + i, n)}, device_id_type=MESH)
 
@@ -73,7 +77,9 @@
         wide = jnp.dot(piece, spread, preferred_element_type=F32)
         weights[term] = jnp.where(taken, wide, 0.0).astype(BF16)
 
-    pl.semaphore_wait(barrier, n_ep - 1 + n - 1)
+    pl.semaphore_wait(barrier, count - 1 + len(column) + n - 1)
+    for peer in column:
+        pl.semaphore_signal(row_sem, inc=1, device_id={"ep": peer}, device_id_type=MESH)
 
     def to_columns(i):
         to = lax.rem(me + i, n)
@@ -124,6 +130,7 @@
         send[blocks(g)] = x.astype(BF16).reshape(2 * per, cap, width)
         if g == 0:
             keep_rows.start()
+            pl.semaphore_wait(row_sem, len(column))
 
         @pl.loop(max(1, 2 * per * g), 2 * per * (g + 1))
         def _(i):
@@ -317,7 +324,7 @@
             pltpu.VMEM((chunks, 8, part), F32),
             pltpu.VMEM((chunks, part, width), F32),
             pltpu.VMEM((n, tok // n, width), BF16),
-            dma((7,)), dma((n,)), dma((n,)), dma((n,)), dma((n,)), dma((n_ep,)), dma((n_ep,)), dma((n,)), dma((n,)),
+            pltpu.SemaphoreType.REGULAR, dma((7,)), dma((n,)), dma((n,)), dma((n,)), dma((n,)), dma((n_ep,)), dma((n_ep,)), dma((n,)), dma((n,)),
             dma((n_ep,)), dma((n_ep,)), ring, ring, ring, ring,
         ],
         compiler_params=pltpu.CompilerParams(collective_id=0, has_side_effects=True, vmem_limit_bytes=48 * 2**20),

time: 134 us -> 132 us (0.985)
  Pallas kernels: 128 us -> 126 us
    pallas_call x1, Pallas kernels: 128 us -> 126 us  [per_device(): pl.pallas_call(functools.partial(layer_kernel, n_ep, n, cap), out_shape=j...]
where the time goes in v5:
time: 132 us
  Pallas kernels  126 us (95%)
  local copies, waits for them, and re-layouts  5.57 us (4%)
    pallas_call x1, Pallas kernels, per_device(): pl.pallas_call(functools.partial(layer_kernel, n_ep, n, cap), out_shape=j...  126 us
    unnamed x17, local copies, waits for them, and re-layouts  5.57 us

profile of v5, /device:TPU:1, one launch (start us, length us, event | category | flops | bytes accessed | tf_op | source)
XLA Modules:
  0.0 131.7 jit_solution(5451795971104379074)
XLA Ops:
  0.0 0.0 copy-start.6
  0.0 0.7 copy-done.6
  0.7 0.0 copy-start.3
  0.7 0.0 copy-start.4
  0.7 0.1 copy.9.ids
  0.8 0.0 copy-start.5
  0.8 0.8 copy.10.gates
  1.6 0.0 copy-done.3
  1.6 0.0 copy-done.4
  1.6 0.0 copy-done.5
  1.6 0.0 copy-start
  1.6 1.1 copy-done
  2.8 0.0 copy-start.1
  2.8 1.1 copy-done.1
  3.9 0.0 copy-start.2
  3.9 1.1 copy-done.2
  5.0 126.1 %shard_map.82 = bf16[16,2048]{1,0:T(8,128)(2,1)S(1)} custom-call(bf16[128,256]{1,0:T(8,128)(2,1)S(1)} %copy-done.3, bf16[16,2048]{1,0:T(8,128)(2,1)S(1)} %copy-done.4, f32[1,2048]{1,0:T(1,128)S(1)} %bitcast.7, s32[128,6]{1,0:T(8,128)S(1)} %copy.9.ids, f32[128,6]{1,0:T(8,128)S(1)} %copy.10.gates, bf16[176,2048]{1,0:T(8,128)(2,1)S(1)} %bitcast.4, ...), custom_call_target="tpu_custom_call" | custom-call | tf_op jit(solution)/shard_map/pallas_call | solution.py:303
  131.1 0.6 copy.12
Async XLA Ops:
  0.0 0.7 copy-start.6
  0.7 0.9 copy-start.3
  0.7 0.9 copy-start.4
  0.8 0.8 copy-start.5
  1.6 1.1 copy-start
  2.8 1.1 copy-start.1
  3.9 1.1 copy-start.2
